TPU v7x, 32 devices: a whole 2x2x4 slice. The times are simulated.
32 devices in a mesh: seq: 4 (over x, core), chan: 8 (over z, y).
Axes of the slice: x: 2, y: 2, z: 4, core: 2. Of those that a mesh axis runs over, the one named last changes fastest.
Arguments:
- features: bfloat16 [3, 4096, 512], P(None, 'chan', 'seq'), may hold values from -6 to 6
- cotangent: bfloat16 [4096, 512], P('chan', 'seq'), may hold values from -6 to 6
- long_filter: bfloat16 [4096, 512], P('chan', 'seq'), may hold values from -0.25 to 0.25
- short_filters: float32 [3, 4096, 3], P(None, 'chan'), may hold values from -3.5 to 3.5
- skip_gain: float32 [4096], P('chan'), may hold values from -4 to 4
Outputs:
- gated_out: bfloat16 [4096, 512], P('chan', 'seq')
- feature_grad: bfloat16 [3, 4096, 512], P(None, 'chan', 'seq')
- long_grad: bfloat16 [4096, 512], P('chan', 'seq')
- short_grad: float32 [3, 4096, 3], P(None, 'chan')
- skip_grad: float32 [4096], P('chan')
All inputs are finite; a program needn't handle non-finite values.
Results may differ from a plain program's by a relative error of at most 0.015.
Values may be sent and summed in bfloat16 or wider, within the bound.
A program may use at most 64 MiB of HBM per device.

v0:
```python
import math

import jax
import jax.numpy as jnp
from jax import lax
from jax.sharding import PartitionSpec as P

inner_length = 128
radix_width = 8


def phase_tables(row_count, col_count, length, direction):
    phase_index = (
        lax.iota(jnp.int32, row_count)[:, None] * lax.iota(jnp.int32, col_count)[None, :] % length
    )
    angles = direction * 2.0 * math.pi / length * phase_index.astype(jnp.float32)
    return (jnp.cos(angles), jnp.sin(angles))


def last_axis(operand, matrix):
    return jnp.einsum("...n,nk->...k", operand, matrix, precision=lax.Precision.HIGH)


def first_axis(operand, matrix):
    return jnp.einsum("...ab,ak->...kb", operand, matrix, precision=lax.Precision.HIGH)


def transform(real_part, imag_part, direction):
    length = real_part.shape[-1]
    if length <= inner_length or length % radix_width != 0:
        cos_table, sin_table = phase_tables(length, length, length, direction)
        return (
            last_axis(real_part, cos_table) - last_axis(imag_part, sin_table),
            last_axis(real_part, sin_table) + last_axis(imag_part, cos_table),
        )
    rest_length = length // radix_width
    grid_shape = real_part.shape[:-1] + (radix_width, rest_length)
    real_grid = real_part.reshape(grid_shape)
    imag_grid = imag_part.reshape(grid_shape)
    cos_table, sin_table = phase_tables(radix_width, radix_width, radix_width, direction)
    section_real = first_axis(real_grid, cos_table) - first_axis(imag_grid, sin_table)
    section_imag = first_axis(real_grid, sin_table) + first_axis(imag_grid, cos_table)
    twist_cos, twist_sin = phase_tables(radix_width, rest_length, length, direction)
    turned_real = section_real * twist_cos - section_imag * twist_sin
    turned_imag = section_real * twist_sin + section_imag * twist_cos
    inner_real, inner_imag = transform(turned_real, turned_imag, direction)
    return (
        jnp.swapaxes(inner_real, -1, -2).reshape(real_part.shape),
        jnp.swapaxes(inner_imag, -1, -2).reshape(real_part.shape),
    )


def spectral(mixed_term, gated_grad, kernel, local_gain):
    length = mixed_term.shape[-1]
    mixed_wide = mixed_term.astype(jnp.float32)
    gated_wide = gated_grad.astype(jnp.float32)
    kernel_wide = kernel.astype(jnp.float32)
    extend = ((0, 0), (0, length))
    real_in = jnp.stack([jnp.pad(mixed_wide, extend), jnp.pad(kernel_wide, extend)])
    imag_in = jnp.stack(
        [jnp.pad(gated_wide, extend), jnp.zeros((kernel_wide.shape[0], 2 * length), jnp.float32)]
    )
    freq_real, freq_imag = transform(real_in, imag_in, -1.0)
    packed_real = freq_real[0]
    packed_imag = freq_imag[0]
    mirror_real = jnp.roll(jnp.flip(packed_real, -1), 1, -1)
    mirror_imag = jnp.roll(jnp.flip(packed_imag, -1), 1, -1)
    mix_real = 0.5 * (packed_real + mirror_real)
    mix_imag = 0.5 * (packed_imag - mirror_imag)
    grad_real = 0.5 * (packed_imag + mirror_imag)
    grad_imag = 0.5 * (mirror_real - packed_real)
    kern_real = freq_real[1]
    kern_imag = freq_imag[1]
    conv_real = mix_real * kern_real - mix_imag * kern_imag
    conv_imag = mix_real * kern_imag + mix_imag * kern_real
    corr_real = grad_real * kern_real + grad_imag * kern_imag
    corr_imag = grad_imag * kern_real - grad_real * kern_imag
    cross_real = grad_real * mix_real + grad_imag * mix_imag
    cross_imag = grad_imag * mix_real - grad_real * mix_imag
    back_real = jnp.stack([conv_real - corr_imag, cross_real])
    back_imag = jnp.stack([conv_imag + corr_real, cross_imag])
    time_real, time_imag = transform(back_real, back_imag, 1.0)
    inverse_scale = 1.0 / (2 * length)
    conv_part = time_real[0, :, :length] * inverse_scale
    corr_part = time_imag[0, :, :length] * inverse_scale
    cross_part = time_real[1, :, :length] * inverse_scale
    gain_column = local_gain[:, None]
    long_out = (conv_part + gain_column * mixed_wide).astype(jnp.bfloat16)
    mixed_grad = (corr_part + gain_column * gated_wide).astype(jnp.bfloat16)
    return (long_out, mixed_grad, cross_part.astype(jnp.bfloat16))


def featurize(history, weights, margin, span_count):
    running = weights[:, :, 0:1] * history[:, :, margin : margin + span_count]
    for offset in range(1, margin + 1):
        running = (
            running
            + weights[:, :, offset : offset + 1]
            * history[:, :, margin - offset : margin - offset + span_count]
        )
    return running


def unfeaturize(padded_grad, weights, span_count):
    running = weights[:, :, 0:1] * padded_grad[:, :, 0:span_count]
    for offset in range(1, weights.shape[2]):
        running = (
            running
            + weights[:, :, offset : offset + 1] * padded_grad[:, :, offset : offset + span_count]
        )
    return running


def tap_grads(primed_grad, history, margin, span_count):
    columns = []
    for offset in range(margin + 1):
        columns.append(
            jnp.sum(
                primed_grad * history[:, :, margin - offset : margin - offset + span_count], axis=-1
            )
        )
    return jnp.stack(columns, axis=-1)


def shards(features, cotangent, long_filter, short_filters, skip_gain):
    groups = lax.axis_size("seq")
    seq_index = lax.axis_index("seq")
    channels = features.shape[1]
    per_group = channels // groups
    margin = short_filters.shape[2] - 1
    local_gain = lax.dynamic_slice_in_dim(skip_gain, seq_index * per_group, per_group, 0)
    stacked = jnp.concatenate([features, cotangent[None], long_filter[None]], 0)
    columns = lax.all_to_all(stacked, "seq", split_axis=1, concat_axis=2, tiled=True)
    weights = lax.dynamic_slice_in_dim(short_filters, seq_index * per_group, per_group, 1)
    length = columns.shape[2]
    history = jnp.pad(columns[:3].astype(jnp.float32), ((0, 0), (0, 0), (margin, 0)))
    primed = featurize(history, weights, margin, length)
    mixed_term = (primed[1] * primed[2]).astype(jnp.bfloat16)
    cot_wide = columns[3].astype(jnp.float32)
    gated_grad = (cot_wide * primed[0]).astype(jnp.bfloat16)
    long_out, mixed_grad, kernel_grad = spectral(mixed_term, gated_grad, columns[4], local_gain)
    long_wide = long_out.astype(jnp.float32)
    mixed_back = mixed_grad.astype(jnp.float32)
    gated_out = (primed[0] * long_wide).astype(jnp.bfloat16)
    primed_grad = jnp.stack([cot_wide * long_wide, mixed_back * primed[2], mixed_back * primed[1]])
    padded_grad = jnp.pad(primed_grad, ((0, 0), (0, 0), (0, margin)))
    feature_grad = unfeaturize(padded_grad, weights, length).astype(jnp.bfloat16)
    taps_grad = tap_grads(primed_grad, history, margin, length)
    gain_grad = jnp.sum(gated_grad.astype(jnp.float32) * mixed_term.astype(jnp.float32), axis=-1)
    results = jnp.concatenate([gated_out[None], feature_grad, kernel_grad[None]], 0)
    row_blocks = lax.all_to_all(results, "seq", split_axis=2, concat_axis=1, tiled=True)
    short_grad, skip_grad = (
        lax.all_gather(taps_grad, "seq", axis=1, tiled=True),
        lax.all_gather(gain_grad, "seq", axis=0, tiled=True),
    )
    return (row_blocks[0], row_blocks[1:4], row_blocks[4], short_grad, skip_grad)


def solution(mesh):
    placed = (
        P(None, "chan", "seq"),
        P("chan", "seq"),
        P("chan", "seq"),
        P(None, "chan", None),
        P("chan"),
    )
    return jax.shard_map(
        shards,
        mesh=mesh,
        in_specs=placed,
        out_specs=(
            P("chan", "seq"),
            P(None, "chan", "seq"),
            P("chan", "seq"),
            P(None, "chan", None),
            P("chan"),
        ),
        check_vma=False,
    )
```

profile of v0, /device:TPU:0, one launch (start us, length us, event | category | flops | bytes accessed | tf_op | source)
XLA Modules:
  0.0 104.6 jit_solution(2643128398959037245)
XLA Ops:
  0.6 1.2 %copy.108 = bf16[1,512,128]{2,0,1:T(2,128)(2,1)S(1)} copy(bf16[1,512,128]{2,1,0:T(8,128)(2,1)} %bitcast.192) | data formatting | bytes 262144 | tf_op jit(solution)/shard_map/broadcast_in_dim | solution.py:132
  1.8 1.1 %copy.107 = bf16[1,512,128]{2,0,1:T(2,128)(2,1)S(1)} copy(bf16[1,512,128]{2,1,0:T(8,128)(2,1)} %bitcast.193) | data formatting | bytes 262144 | tf_op jit(solution)/shard_map/broadcast_in_dim | solution.py:132
  3.3 1.9 %pad_maximum_fusion = bf16[5,512,128]{2,0,1:T(8,128)(2,1)} fusion(bf16[1,512,128]{2,0,1:T(2,128)(2,1)S(1)} %copy.108, bf16[1,512,128]{2,0,1:T(2,128)(2,1)S(1)} %copy.107, bf16[3,512,128]{2,0,1:T(4,128)(2,1)S(1)} %copy.106), kind=kLoop, calls=%fused_computation.12 | loop fusion | flops 1966080 | bytes 1310720 | tf_op jit(solution)/shard_map/concatenate | solution.py:132
  5.1 4.2 %all-to-all-start = ((bf16[5,512,128]{2,0,1:T(8,128)(2,1)}), bf16[5,512,128]{2,0,1:T(8,128)(2,1)S(1)}, u32[]{:S(2)}, u32[]{:S(2)}) async-start(bf16[5,512,128]{2,0,1:T(8,128)(2,1)} %pad_maximum_fusion), calls=%async_computation | async-start | bytes 2097152 | tf_op jit(solution)/shard_map/all_to_all | solution.py:133
  9.4 0.9 constant_dynamic-slice_fusion.1
  10.3 1.3 %dynamic_slice.7 = f32[128]{0:T(128)} dynamic-slice(f32[512]{0:T(512)} %param.9, s32[]{:T(128)S(6)} %select_n.84), dynamic_slice_sizes={128} | dynamic-slice | bytes 1028 | tf_op jit(solution)/shard_map/dynamic_slice | solution.py:131
  11.6 0.7 multiply_sine_fusion.7
  12.9 10.9 %all-to-all-done = bf16[5,512,128]{2,0,1:T(8,128)(2,1)S(1)} async-done(((bf16[5,512,128]{2,0,1:T(8,128)(2,1)}), bf16[5,512,128]{2,0,1:T(8,128)(2,1)S(1)}, u32[]{:S(2)}, u32[]{:S(2)}) %all-to-all-start) | async-done | bytes 655392 | tf_op jit(solution)/shard_map/all_to_all | solution.py:133
  25.7 1.3 %multiply_reduce_fusion.2 = (f32[128]{0:T(128)}, f32[128,512]{0,1:T(8,128)}, bf16[1,128,512]{1,2,0:T(8,128)(2,1)S(1)}) fusion(f32[3,128,512]{1,2,0:T(8,128)S(1)} %multiply_add_fusion, f32[1,128,4,128]{1,3,2,0:T(8,128)S(1)} %get-tuple-element.51), kind=kLoop, calls=%fused_computation.80 | loop fusion | flops 524160 | bytes 1442304 | tf_op jit(solution)/shard_map/reduce_sum | solution.py:149
  27.3 1.6 %fusion.18 = f32[8,2,128,128]{3,0,2,1:T(8,128)} fusion(f32[1,128,8,128]{3,2,1,0:T(8,128)S(1)} %bitcast.169, f32[1,128,8,128]{3,2,1,0:T(8,128)S(1)} %copy.156), kind=kOutput, calls=%fused_computation.36 | convolution fusion | flops 12845952 | bytes 2097152 | tf_op jit(solution)/shard_map/...ab,ak->...kb/dot_general | solution.py:25
  28.9 1.6 %fusion.19 = f32[8,2,128,128]{3,0,2,1:T(8,128)} fusion(f32[1,128,8,128]{3,2,1,0:T(8,128)S(1)} %bitcast.170, f32[1,128,8,128]{3,2,1,0:T(8,128)S(1)} %copy.156), kind=kOutput, calls=%fused_computation.37 | convolution fusion | flops 12845952 | bytes 2097152 | tf_op jit(solution)/shard_map/...ab,ak->...kb/dot_general | solution.py:25
  30.5 1.1 %stack.58 = f32[2,128,1024]{1,2,0:T(8,128)} pad(f32[1,128,1024]{1,2,0:T(8,128)S(1)} %pad_bitcast_fusion, f32[]{:T(128)} %constant.67.clone.1), padding=0_1x0_0x0_0 | pad | bytes 1572868 | tf_op jit(solution)/shard_map/stack | solution.py:60
  31.6 1.6 %copy.158 = f32[2,128,8,128]{3,2,1,0:T(8,128)S(1)} copy(f32[2,128,8,128]{1,3,2,0:T(8,128)} %bitcast.176) | data formatting | bytes 2097152 | tf_op jit(solution)/shard_map/reshape | solution.py:39
  33.2 1.9 %convolution_add_fusion.3 = f32[8,2,128,128]{3,0,2,1:T(8,128)S(1)} fusion(f32[8,2,128,128]{3,0,2,1:T(8,128)} %fusion.18, f32[2,128,8,128]{3,2,1,0:T(8,128)S(1)} %copy.158), kind=kOutput, calls=%fused_computation.10 | convolution fusion | flops 12845952 | bytes 3145728 | tf_op jit(solution)/shard_map/...ab,ak->...kb/dot_general | solution.py:25
  35.2 0.8 add_bitcast_fusion.1
  36.0 0.9 fusion.12
  36.9 0.9 fusion.14
  37.8 0.9 fusion.3
  38.6 0.9 fusion.168
  39.8 0.9 slice.152
  41.2 0.9 fusion.2
  42.5 0.8 slice.156
  43.8 1.1 %copy.127 = f32[1,128,128,8]{1,3,2,0:T(8,128)} copy(f32[1,128,128,8]{1,2,3,0:T(8,128)S(1)} %get-tuple-element.45) | data formatting | bytes 1048576 | tf_op jit(solution)/shard_map/slice | solution.py:73
  44.9 1.3 %copy.128 = f32[1,128,8,128]{3,2,1,0:T(8,128)S(1)} copy(f32[1,128,8,128]{1,3,2,0:T(8,128)} %bitcast.187) | data formatting | bytes 1048576 | tf_op jit(solution)/shard_map/squeeze | solution.py:73
  46.2 2.2 %copy.119 = f32[1,128,128,8]{1,3,2,0:T(8,128)} copy(f32[1,128,128,8]{1,2,3,0:T(8,128)} %get-tuple-element.47) | data formatting | bytes 1048576 | tf_op jit(solution)/shard_map/slice | solution.py:72
  48.4 2.0 %copy.120 = f32[1,128,8,128]{3,2,1,0:T(8,128)} copy(f32[1,128,8,128]{1,3,2,0:T(8,128)} %bitcast.188) | data formatting | bytes 1048576 | tf_op jit(solution)/shard_map/squeeze | solution.py:72
  50.4 1.0 copy.118
  51.4 3.7 %slice.128 = f32[128,1023]{0,1:T(8,128)S(1)} reverse(f32[128,1023]{0,1:T(8,128)} %slice.152), dimensions={1} | reverse | bytes 1047552 | tf_op jit(solution)/shard_map/jit(_roll_static)/slice | solution.py:66
  55.2 1.5 %pad_maximum_fusion.12 = f32[1,128,1024]{1,2,0:T(8,128)} fusion(f32[1,128,1023]{1,2,0:T(8,128)S(1)} %bitcast.182, f32[1,128,1]{1,2,0:T(1,128)} %slice_bitcast_fusion.1), kind=kLoop, calls=%fused_computation.48 | loop fusion | flops 131072 | bytes 1048576 | tf_op jit(solution)/shard_map/jit(_roll_static)/concatenate | solution.py:66
  56.6 2.1 %copy.159 = f32[1,128,8,128]{3,2,1,0:T(8,128)} copy(f32[1,128,8,128]{1,3,2,0:T(8,128)} %bitcast.183) | data formatting | bytes 1048576 | tf_op jit(solution)/shard_map/jit(_roll_static)/concatenate | solution.py:66
  58.8 1.0 copy.126
  59.8 0.7 slice.133
  60.5 1.5 %pad_maximum_fusion.13 = f32[1,128,1024]{1,2,0:T(8,128)} fusion(f32[1,128,1023]{1,2,0:T(8,128)S(1)} %bitcast.184, f32[1,128,1]{1,2,0:T(1,128)} %slice_bitcast_fusion), kind=kLoop, calls=%fused_computation.49 | loop fusion | flops 131072 | bytes 1048576 | tf_op jit(solution)/shard_map/jit(_roll_static)/concatenate | solution.py:67
  62.1 2.1 %copy.160 = f32[1,128,8,128]{3,2,1,0:T(8,128)} copy(f32[1,128,8,128]{1,3,2,0:T(8,128)} %bitcast.185) | data formatting | bytes 1048576 | tf_op jit(solution)/shard_map/jit(_roll_static)/concatenate | solution.py:67
  64.2 1.6 %add_add_fusion = (f32[1,128,8,128]{3,2,1,0:T(8,128)S(1)}, f32[1,128,8,128]{3,2,1,0:T(8,128)S(1)}, f32[1,128,8,128]{3,2,1,0:T(8,128)S(1)}, f32[1,128,8,128]{3,2,1,0:T(8,128)S(1)}, f32[1,128,8,128]{3,2,1,0:T(8,128)S(1)}) fusion(f32[1,128,8,128]{3,2,1,0:T(8,128)S(1)} %copy.128, f32[1,128,8,128]{3,2,1,0:T(8,128)S(1)} %copy-done, ...), kind=kLoop, calls=%fused_computation.52 | loop fusion | flops 1966080 | bytes 5767168 | tf_op jit(solution)/shard_map/add | solution.py:81
  67.4 0.7 convolution_add_fusion.1
  68.0 0.9 add_bitcast_fusion
  68.9 0.9 fusion.8
  69.8 0.9 fusion.6
  70.7 0.9 fusion.1
  72.2 0.9 fusion
  74.5 1.5 %copy.143 = bf16[5,128,512]{1,0,2:T(8,128)(2,1)} copy(bf16[5,128,512]{1,2,0:T(8,128)(2,1)S(1)} %pad_maximum_fusion.11) | data formatting | bytes 1310720 | tf_op jit(solution)/shard_map/concatenate | solution.py:150
  76.0 3.6 %all-to-all-start.1 = ((bf16[5,128,512]{1,0,2:T(8,128)(2,1)}), bf16[5,128,512]{1,0,2:T(8,128)(2,1)S(1)}, u32[]{:S(2)}, u32[]{:S(2)}) async-start(bf16[5,128,512]{1,0,2:T(8,128)(2,1)} %copy.143), calls=%async_computation.1 | async-start | bytes 2097152 | tf_op jit(solution)/shard_map/all_to_all | solution.py:151
  79.8 15.3 %all_gather.6 = f32[3,512,3]{1,0,2:T(4,128)S(1)} all-gather(f32[3,128,3]{1,0,2:T(4,128)S(1)} %pad_maximum_fusion.14), channel_id=1, replica_groups=mesh['seq'=4,'chan'=8] {'seq'}, dimensions={1}, use_global_device_ids=true | all-gather | bytes 23040 | tf_op jit(solution)/shard_map/all_gather | solution.py:153
  95.7 5.0 %all-gather = f32[4,1,128]{2,1,0:T(1,128)S(1)} all-gather(f32[1,1,128]{2,1,0:T(1,128)S(1)} %bitcast.202), channel_id=1, replica_groups=mesh['seq'=4,'chan'=8] {'seq'}, dimensions={0}, use_global_device_ids=true | all-gather | bytes 2560 | tf_op jit(solution)/shard_map/all_gather | solution.py:154
  101.4 0.8 copy.144
  102.2 1.0 copy.145
  103.2 0.8 copy.146
  (64 shorter events, 10.4 us)
Async XLA Ops:
  0.6 2.3 %copy-start.7 = (bf16[3,512,128]{2,1,0:T(8,128)(2,1)S(1)}, bf16[3,512,128]{2,1,0:T(8,128)(2,1)}, u32[]{:S(2)}) copy-start(bf16[3,512,128]{2,1,0:T(8,128)(2,1)} %param.5) | copy-start | bytes 1179652
  5.1 18.7 %all-to-all-start = ((bf16[5,512,128]{2,0,1:T(8,128)(2,1)}), bf16[5,512,128]{2,0,1:T(8,128)(2,1)S(1)}, u32[]{:S(2)}, u32[]{:S(2)}) async-start(bf16[5,512,128]{2,0,1:T(8,128)(2,1)} %pad_maximum_fusion), calls=%async_computation | async-start | bytes 2097152 | tf_op jit(solution)/shard_map/all_to_all | solution.py:133
  24.5 0.8 copy-start.1
  28.9 1.6 %copy-start.6 = (f32[128,512]{0,1:T(8,128)S(1)}, f32[128,512]{0,1:T(8,128)}, u32[]{:S(2)}) copy-start(f32[128,512]{0,1:T(8,128)} %get-tuple-element.23) | copy-start | bytes 786436
  33.2 2.0 %copy-start.3 = (f32[8,2,128,128]{3,0,2,1:T(8,128)S(1)}, f32[8,2,128,128]{3,0,2,1:T(8,128)}, u32[]{:S(2)}) copy-start(f32[8,2,128,128]{3,0,2,1:T(8,128)} %fusion.19) | copy-start | bytes 3145732
  33.2 2.0 %copy-start.9 = (f32[8,128]{1,0:T(8,128)S(1)}, f32[8,128]{1,0:T(8,128)}, u32[]{:S(2)}) copy-start(f32[8,128]{1,0:T(8,128)} %get-tuple-element.62) | copy-start | bytes 12292
  33.2 2.0 %copy-start.10 = (f32[8,128]{1,0:T(8,128)S(1)}, f32[8,128]{1,0:T(8,128)}, u32[]{:S(2)}) copy-start(f32[8,128]{1,0:T(8,128)} %get-tuple-element.63) | copy-start | bytes 12292
  56.6 3.1 %copy-start.4 = (f32[128,1023]{0,1:T(8,128)S(1)}, f32[128,1023]{0,1:T(8,128)}, u32[]{:S(2)}) copy-start(f32[128,1023]{0,1:T(8,128)} %slice.156) | copy-start | bytes 1571332
  60.5 3.7 %copy-start = (f32[1,128,8,128]{3,2,1,0:T(8,128)S(1)}, f32[1,128,8,128]{3,2,1,0:T(8,128)}, u32[]{:S(2)}) copy-start(f32[1,128,8,128]{3,2,1,0:T(8,128)} %copy.120) | copy-start | bytes 1572868
  62.1 2.1 %copy-start.5 = (f32[1,128,8,128]{3,2,1,0:T(8,128)S(1)}, f32[1,128,8,128]{3,2,1,0:T(8,128)}, u32[]{:S(2)}) copy-start(f32[1,128,8,128]{3,2,1,0:T(8,128)} %copy.118) | copy-start | bytes 1572868
  67.3 0.7 copy-start.8
  73.1 0.7 copy-start.12
  76.0 3.7 %copy-start.2 = (bf16[5,4,128,128]{2,3,1,0:T(8,128)(2,1)S(1)}, bf16[5,4,128,128]{2,3,1,0:T(8,128)(2,1)}, u32[]{:S(2)}) copy-start(bf16[5,4,128,128]{2,3,1,0:T(8,128)(2,1)} %copy-done.1) | copy-start | bytes 1966084
  76.0 24.7 %all-to-all-start.1 = ((bf16[5,128,512]{1,0,2:T(8,128)(2,1)}), bf16[5,128,512]{1,0,2:T(8,128)(2,1)S(1)}, u32[]{:S(2)}, u32[]{:S(2)}) async-start(bf16[5,128,512]{1,0,2:T(8,128)(2,1)} %copy.143), calls=%async_computation.1 | async-start | bytes 2097152 | tf_op jit(solution)/shard_map/all_to_all | solution.py:151
  79.6 16.0 %copy-start.11 = (f32[128]{0:T(128)S(1)}, f32[128]{0:T(128)}, u32[]{:S(2)}) copy-start(f32[128]{0:T(128)} %get-tuple-element.22) | copy-start | bytes 1540
where the time goes:
time: 105 us
  local copies, waits for them, and re-layouts  38.1 us (36%)
  blocking collectives  20.3 us (19%)
  matrix products  15.7 us (15%)
  waiting for transfers between devices  10.9 us (10%)
  other arithmetic  10.6 us (10%)
  starting transfers between devices  7.88 us (8%)
  between operations  1.1 us (1%)
    all_gather x1, blocking collectives, shards(): lax.all_gather(taps_grad, 'seq', axis=1, tiled=True)  15.3 us
    all_to_all x1, waiting for transfers between devices, shards(): lax.all_to_all(stacked, 'seq', split_axis=1, concat_axis=2, tiled=True)  10.9 us
    dot_general x8, matrix products, first_axis(): jnp.einsum('...ab,ak->...kb', operand, matrix, precision=lax.Precision.HIGH)  8.77 us
    dot_general x8, matrix products, last_axis(): jnp.einsum('...n,nk->...k', operand, matrix, precision=lax.Precision.HIGH)  6.96 us
    all_gather x1, blocking collectives, shards(): lax.all_gather(gain_grad, 'seq', axis=0, tiled=True)  5.05 us
    slice x2, local copies, waits for them, and re-layouts, spectral(): mirror_real = jnp.roll(jnp.flip(packed_real, -1), 1, -1)  4.57 us
    all_to_all x1, starting transfers between devices, shards(): lax.all_to_all(stacked, 'seq', split_axis=1, concat_axis=2, tiled=True)  4.24 us
    all_to_all x1, starting transfers between devices, shards(): lax.all_to_all(results, 'seq', split_axis=2, concat_axis=1, tiled=True)  3.65 us
  transfers between devices with their start and end apart: 2, of which 1 were waited for; matrix products, arithmetic and copies ran while one was open for 4% of the time, Pallas kernels for 0%

commit v1 on v0

--- a/solution.py
+++ b/solution.py
@@ -1,12 +1,17 @@
+import functools
 import math
 
 import jax
 import jax.numpy as jnp
+import numpy as np
 from jax import lax
+from jax.experimental import pallas as pl
+from jax.experimental.pallas import tpu as pltpu
 from jax.sharding import PartitionSpec as P
 
 inner_length = 128
 radix_width = 8
+chunk_count = 1
 
 
 def phase_tables(row_count, col_count, length, direction):
@@ -122,8 +127,398 @@
     return jnp.stack(columns, axis=-1)
 
 
+def packed_tables(length):
+    steps = np.arange(length)
+    phase = (steps[:, None] * steps[None, :]) % (2 * length)
+    angles = np.pi / length * phase
+    sines = np.sin(angles)
+    sines[:, 0] = 1.0 - 2.0 * (steps % 2)
+    table = np.concatenate([np.cos(angles), sines], 1).astype(np.float32)
+    high = table.astype(jnp.bfloat16)
+    low = (table - high.astype(np.float32)).astype(jnp.bfloat16)
+    return np.stack([high, low])
+
+
+def fused_kernel(
+    sizes,
+    feat_hbm,
+    cot_hbm,
+    filt_hbm,
+    coef_hbm,
+    table_hbm,
+    gated_hbm,
+    grad_hbm,
+    long_hbm,
+    small_hbm,
+    table,
+    coef_rows,
+    coef_cols,
+    arrived,
+    stacked,
+    primed_buf,
+    freq,
+    back_high,
+    back_low,
+    back_time,
+    results,
+    sums,
+    sums_out,
+    load_sem,
+    own_in,
+    own_out,
+    in_send,
+    in_recv,
+    out_send,
+    out_recv,
+    small_own,
+    small_send,
+    small_recv,
+):
+    groups, rows, span, length, taps, chunks = sizes
+    chunk_rows = rows // chunks
+    me = lax.axis_index("seq")
+
+    def at(index, extent):
+        return pl.ds(pl.multiple_of(index * extent, extent), extent)
+
+    def chan_rows(owner, chunk):
+        start = owner * rows + chunk * chunk_rows
+        return pl.ds(pl.multiple_of(start, chunk_rows), chunk_rows)
+
+    loads = [
+        pltpu.make_async_copy(coef_hbm.at[:, at(me, rows)], coef_rows.at[0:16, :], load_sem.at[0]),
+        pltpu.make_async_copy(table_hbm, table, load_sem.at[1]),
+    ]
+    for load in loads:
+        load.start()
+
+    def in_pairs(owner, source, chunk):
+        taken = chan_rows(owner, chunk)
+        kept = pl.ds(chunk * chunk_rows, chunk_rows)
+        tokens = at(source, span)
+        return [
+            (filt_hbm.at[taken, :], arrived.at[4, kept, tokens]),
+            (feat_hbm.at[:, taken, :], arrived.at[0:3, kept, tokens]),
+            (cot_hbm.at[taken, :], arrived.at[3, kept, tokens]),
+        ]
+
+    def out_pairs(target, owner, chunk):
+        kept = pl.ds(chunk * chunk_rows, chunk_rows)
+        placed = chan_rows(owner, chunk)
+        tokens = at(target, span)
+        return [
+            (results.at[0, kept, tokens], gated_hbm.at[placed, :]),
+            (results.at[1:4, kept, tokens], grad_hbm.at[:, placed, :]),
+            (results.at[4, kept, tokens], long_hbm.at[placed, :]),
+        ]
+
+    def remote(pair, send_sem, recv_sem, peer):
+        return pltpu.make_async_remote_copy(
+            src_ref=pair[0],
+            dst_ref=pair[1],
+            send_sem=send_sem,
+            recv_sem=recv_sem,
+            device_id={"seq": peer},
+            device_id_type=pl.DeviceIdType.MESH,
+        )
+
+    own_copies = []
+    for chunk in range(chunks):
+        for kind, pair in enumerate(in_pairs(me, me, chunk)):
+            copy = pltpu.make_async_copy(pair[0], pair[1], own_in.at[chunk, kind])
+            copy.start()
+            own_copies.append(copy)
+
+    barrier = pltpu.get_barrier_semaphore()
+    for offset in range(1, groups):
+        pl.semaphore_signal(
+            barrier,
+            inc=1,
+            device_id={"seq": lax.rem(me + offset, groups)},
+            device_id_type=pl.DeviceIdType.MESH,
+        )
+    pl.semaphore_wait(barrier, groups - 1)
+
+    sent = []
+    for chunk in range(chunks):
+        for offset in range(1, groups):
+            peer = lax.rem(me + offset, groups)
+            for kind, pair in enumerate(in_pairs(peer, me, chunk)):
+                copy = remote(
+                    pair, in_send.at[chunk, kind, offset], in_recv.at[chunk, kind, offset], peer
+                )
+                copy.start()
+                sent.append(copy)
+
+    loads[0].wait()
+    coef_rows[16:, :] = jnp.zeros((coef_rows.shape[0] - 16, rows), jnp.float32)
+    coef_cols[...] = coef_rows[...].T
+    loads[1].wait()
+
+    group_rows = 16
+    scale = 1.0 / length
+
+    def column(index, picked):
+        return coef_cols[picked, index : index + 1]
+
+    def delayed(values, offset):
+        if offset == 0:
+            return values
+        lane = lax.broadcasted_iota(jnp.int32, values.shape, 1)
+        return jnp.where(lane >= offset, pltpu.roll(values, offset, 1), 0.0)
+
+    def advanced(values, offset):
+        if offset == 0:
+            return values
+        lane = lax.broadcasted_iota(jnp.int32, values.shape, 1)
+        moved = pltpu.roll(values, length - offset, 1)
+        return jnp.where(lane < length - offset, moved, 0.0)
+
+    for chunk in range(chunks):
+        base = chunk * chunk_rows
+        for kind in range(3):
+            own_copies[chunk * 3 + kind].wait()
+        for offset in range(1, groups):
+            source = lax.rem(me + groups - offset, groups)
+            for kind, pair in enumerate(in_pairs(me, source, chunk)):
+                remote(
+                    pair, in_send.at[chunk, kind, offset], in_recv.at[chunk, kind, offset], source
+                ).wait_recv()
+
+        @pl.loop(0, chunk_rows // group_rows)
+        def _(step):
+            inner = pl.ds(pl.multiple_of(step * group_rows, group_rows), group_rows)
+            picked = pl.ds(pl.multiple_of(base + step * group_rows, group_rows), group_rows)
+            primed = []
+            for stream in range(3):
+                wide = arrived[stream, picked, :].astype(jnp.float32)
+                running = column(stream * taps, picked) * wide
+                for offset in range(1, taps):
+                    running = running + column(stream * taps + offset, picked) * delayed(
+                        wide, offset
+                    )
+                primed.append(running)
+                primed_buf[stream, inner, :] = running
+            stacked[0, inner, :] = (primed[1] * primed[2]).astype(jnp.bfloat16)
+            cot_wide = arrived[3, picked, :].astype(jnp.float32)
+            stacked[1, inner, :] = (cot_wide * primed[0]).astype(jnp.bfloat16)
+            stacked[2, inner, :] = arrived[4, picked, :]
+
+        tile = 256
+
+        @pl.loop(0, 2 * length // tile)
+        def _(step):
+            columns = pl.ds(pl.multiple_of(step * tile, tile), tile)
+            left = stacked[...].reshape(3 * chunk_rows, length)
+            total = jnp.dot(left, table[0, :, columns], preferred_element_type=jnp.float32)
+            total += jnp.dot(left, table[1, :, columns], preferred_element_type=jnp.float32)
+            freq[:, :, columns] = total.reshape(3, chunk_rows, tile)
+
+        @pl.loop(0, chunk_rows // group_rows)
+        def _(step):
+            inner = pl.ds(pl.multiple_of(step * group_rows, group_rows), group_rows)
+            first = lax.broadcasted_iota(jnp.int32, (group_rows, length), 1) == 0
+            weight = jnp.where(first, 0.5 * scale, scale)
+            mix_c, mix_s = freq[0, inner, :length], freq[0, inner, length:]
+            grad_c, grad_s = freq[1, inner, :length], freq[1, inner, length:]
+            kern_c, kern_s = freq[2, inner, :length], freq[2, inner, length:]
+
+            def put(slot, left_c, left_s, right_c, right_s, sign):
+                both = left_s * right_s
+                even = left_c * right_c + sign * jnp.where(first, 0.0, both)
+                odd = jnp.where(first, both, left_s * right_c - sign * (left_c * right_s))
+                for half, part in enumerate((even, odd)):
+                    value = part * weight
+                    high = value.astype(jnp.bfloat16)
+                    low = (value - high.astype(jnp.float32)).astype(jnp.bfloat16)
+                    back_high[slot, inner, half * length : (half + 1) * length] = high
+                    back_low[slot, inner, half * length : (half + 1) * length] = low
+
+            put(0, mix_c, mix_s, kern_c, kern_s, -1.0)
+            put(1, grad_c, grad_s, kern_c, kern_s, 1.0)
+            put(2, grad_c, grad_s, mix_c, mix_s, 1.0)
+
+        @pl.loop(0, length // tile)
+        def _(step):
+            picked = pl.ds(pl.multiple_of(step * tile, tile), tile)
+            high = back_high[...].reshape(3 * chunk_rows, 2 * length)
+            low = back_low[...].reshape(3 * chunk_rows, 2 * length)
+            turned = (((1,), (1,)), ((), ()))
+            total = lax.dot_general(
+                high, table[0, picked, :], turned, preferred_element_type=jnp.float32
+            )
+            total += lax.dot_general(
+                low, table[0, picked, :], turned, preferred_element_type=jnp.float32
+            )
+            total += lax.dot_general(
+                high, table[1, picked, :], turned, preferred_element_type=jnp.float32
+            )
+            back_time[:, :, picked] = total.reshape(3, chunk_rows, tile)
+
+        @pl.loop(0, chunk_rows // group_rows)
+        def _(step):
+            inner = pl.ds(pl.multiple_of(step * group_rows, group_rows), group_rows)
+            picked = pl.ds(pl.multiple_of(base + step * group_rows, group_rows), group_rows)
+            mixed = stacked[0, inner, :].astype(jnp.float32)
+            gated = stacked[1, inner, :].astype(jnp.float32)
+            gain = column(3 * taps, picked)
+            long_wide = (
+                (back_time[0, inner, :] + gain * mixed).astype(jnp.bfloat16).astype(jnp.float32)
+            )
+            mixed_back = (
+                (back_time[1, inner, :] + gain * gated).astype(jnp.bfloat16).astype(jnp.float32)
+            )
+            results[4, picked, :] = back_time[2, inner, :].astype(jnp.bfloat16)
+            results[0, picked, :] = (primed_buf[0, inner, :] * long_wide).astype(jnp.bfloat16)
+            cot_wide = arrived[3, picked, :].astype(jnp.float32)
+            primed_grad = [
+                cot_wide * long_wide,
+                mixed_back * primed_buf[2, inner, :],
+                mixed_back * primed_buf[1, inner, :],
+            ]
+            lane = lax.broadcasted_iota(jnp.int32, (group_rows, sums.shape[1]), 1)
+            line = jnp.zeros((group_rows, sums.shape[1]), jnp.float32)
+            for stream in range(3):
+                moving = primed_grad[stream]
+                wide = arrived[stream, picked, :].astype(jnp.float32)
+                running = column(stream * taps, picked) * moving
+                for offset in range(taps):
+                    if offset:
+                        running = running + column(stream * taps + offset, picked) * advanced(
+                            moving, offset
+                        )
+                    total = jnp.sum(moving * delayed(wide, offset), axis=1, keepdims=True)
+                    line = jnp.where(lane == stream * taps + offset, total, line)
+                results[1 + stream, picked, :] = running.astype(jnp.bfloat16)
+            total = jnp.sum(gated * mixed, axis=1, keepdims=True)
+            sums[picked, :] = jnp.where(lane == 3 * taps, total, line)
+
+        for offset in range(1, groups):
+            peer = lax.rem(me + offset, groups)
+            for kind, pair in enumerate(out_pairs(peer, me, chunk)):
+                copy = remote(
+                    pair, out_send.at[chunk, kind, offset], out_recv.at[chunk, kind, offset], peer
+                )
+                copy.start()
+                sent.append(copy)
+        for kind, pair in enumerate(out_pairs(me, me, chunk)):
+            copy = pltpu.make_async_copy(pair[0], pair[1], own_out.at[chunk, kind])
+            copy.start()
+            own_copies.append(copy)
+
+    sums_out[...] = sums[...].T[0:16, :]
+    own_small = pltpu.make_async_copy(sums_out, small_hbm.at[:, at(me, rows)], small_own)
+    own_small.start()
+    for offset in range(1, groups):
+        peer = lax.rem(me + offset, groups)
+        copy = remote(
+            (sums_out, small_hbm.at[:, at(me, rows)]),
+            small_send.at[offset],
+            small_recv.at[offset],
+            peer,
+        )
+        copy.start()
+        sent.append(copy)
+    for copy in sent:
+        copy.wait_send()
+    for copy in own_copies[3 * chunks :]:
+        copy.wait()
+    own_small.wait()
+    for offset in range(1, groups):
+        source = lax.rem(me + groups - offset, groups)
+        for chunk in range(chunks):
+            for kind, pair in enumerate(out_pairs(me, source, chunk)):
+                remote(
+                    pair, out_send.at[chunk, kind, offset], out_recv.at[chunk, kind, offset], source
+                ).wait_recv()
+        remote(
+            (sums_out, small_hbm.at[:, at(source, rows)]),
+            small_send.at[offset],
+            small_recv.at[offset],
+            source,
+        ).wait_recv()
+
+
+def fused(features, cotangent, long_filter, short_filters, skip_gain, groups, chunks):
+    channels, span = cotangent.shape
+    rows = channels // groups
+    length = span * groups
+    taps = short_filters.shape[2]
+    chunk_rows = rows // chunks
+    coef = jnp.concatenate(
+        [
+            jnp.swapaxes(short_filters, 1, 2).reshape(3 * taps, channels),
+            skip_gain[None],
+            jnp.zeros((15 - 3 * taps, channels), jnp.float32),
+        ],
+        0,
+    )
+    hbm = pl.BlockSpec(memory_space=pl.ANY)
+    dma = pltpu.SemaphoreType.DMA
+    narrow = jnp.bfloat16
+    gated_out, feature_grad, long_grad, small = pl.pallas_call(
+        functools.partial(fused_kernel, (groups, rows, span, length, taps, chunks)),
+        out_shape=(
+            jax.ShapeDtypeStruct((channels, span), narrow),
+            jax.ShapeDtypeStruct((3, channels, span), narrow),
+            jax.ShapeDtypeStruct((channels, span), narrow),
+            jax.ShapeDtypeStruct((16, channels), jnp.float32),
+        ),
+        in_specs=[hbm] * 5,
+        out_specs=(hbm,) * 4,
+        scratch_shapes=[
+            pltpu.VMEM((2, length, 2 * length), narrow),
+            pltpu.VMEM((rows, rows), jnp.float32),
+            pltpu.VMEM((rows, rows), jnp.float32),
+            pltpu.VMEM((5, rows, length), narrow),
+            pltpu.VMEM((3, chunk_rows, length), narrow),
+            pltpu.VMEM((3, chunk_rows, length), jnp.float32),
+            pltpu.VMEM((3, chunk_rows, 2 * length), jnp.float32),
+            pltpu.VMEM((3, chunk_rows, 2 * length), narrow),
+            pltpu.VMEM((3, chunk_rows, 2 * length), narrow),
+            pltpu.VMEM((3, chunk_rows, length), jnp.float32),
+            pltpu.VMEM((5, rows, length), narrow),
+            pltpu.VMEM((rows, rows), jnp.float32),
+            pltpu.VMEM((16, rows), jnp.float32),
+            dma((2,)),
+            dma((chunks, 3)),
+            dma((chunks, 3)),
+            dma((chunks, 3, groups)),
+            dma((chunks, 3, groups)),
+            dma((chunks, 3, groups)),
+            dma((chunks, 3, groups)),
+            dma,
+            dma((groups,)),
+            dma((groups,)),
+        ],
+        compiler_params=pltpu.CompilerParams(
+            collective_id=0, has_side_effects=True, vmem_limit_bytes=48 * 1024 * 1024
+        ),
+    )(features, cotangent, long_filter, coef, packed_tables(length))
+    short_grad = jnp.swapaxes(small[: 3 * taps].reshape(3, taps, channels), 1, 2)
+    return gated_out, feature_grad, long_grad, short_grad, small[3 * taps]
+
+
+def dense_fits(features, short_filters, groups):
+    channels, span = features.shape[1:]
+    rows, length = channels // groups, span * groups
+    return (
+        channels % groups == 0
+        and rows % 128 == 0
+        and span % 128 == 0
+        and length % 256 == 0
+        and length <= 1024
+        and rows <= 256
+        and 3 * short_filters.shape[2] < 16
+    )
+
+
 def shards(features, cotangent, long_filter, short_filters, skip_gain):
     groups = lax.axis_size("seq")
+    if dense_fits(features, short_filters, groups):
+        return fused(
+            features, cotangent, long_filter, short_filters, skip_gain, groups, chunk_count
+        )
     seq_index = lax.axis_index("seq")
     channels = features.shape[1]
     per_group = channels // groups

time: 105 us -> 40.1 us (0.38)
  Pallas kernels: 0 us -> 29.9 us
  local copies, waits for them, and re-layouts: 38.1 us -> 8.48 us
  blocking collectives: 20.3 us -> 0 us
  matrix products: 15.7 us -> 0 us
  waiting for transfers between devices: 10.9 us -> 0 us
  other arithmetic: 10.6 us -> 0.76 us
  starting transfers between devices: 7.88 us -> 0 us
    pallas_call x0 -> x1, Pallas kernels: none -> 29.9 us  [fused(): pl.pallas_call(functools.partial(fused_kernel, (groups, rows, span, lengt...]
    all_gather x2 -> x0, blocking collectives: 20.3 us -> none  [the longest x1 15.3 us: shards(): lax.all_gather(taps_grad, 'seq', axis=1, tiled=True)]
    dot_general x16 -> x0, matrix products: 15.7 us -> none  [the longest x8 8.77 us: first_axis(): jnp.einsum('...ab,ak->...kb', operand, matrix, precision=lax.Precision.HIGH)]
    slice x16 -> x1, local copies, waits for them, and re-layouts: 15.1 us -> 0.58 us  [fused(): return (gated_out, feature_grad, long_grad, short_grad, small[3 * taps])]
    all_to_all x2 -> x0, waiting for transfers between devices: 10.9 us -> none  [the longest x1 10.9 us: shards(): lax.all_to_all(stacked, 'seq', split_axis=1, concat_axis=2, tiled=True)]
    all_to_all x2 -> x0, starting transfers between devices: 7.88 us -> none  [the longest x1 4.24 us: shards(): lax.all_to_all(stacked, 'seq', split_axis=1, concat_axis=2, tiled=True)]
    concatenate x5 -> x1, local copies, waits for them, and re-layouts: 6.71 us -> 0.07 us  [fused(): jnp.concatenate([jnp.swapaxes(short_filters, 1, 2).reshape(3 * taps, chan...]
    squeeze x4 -> x0, local copies, waits for them, and re-layouts: 5.32 us -> none  [the longest x1 2.04 us: spectral(): kern_real = freq_real[1]]
  transfers between devices with their start and end apart: 2 -> 0, of which waited for: 1 -> 0; matrix products, arithmetic and copies ran while one was open for 4% -> 0% of each run, Pallas kernels for 0% -> 0%
where the time goes in v1:
time: 40.1 us; the launch traced here: 39.7 us
  Pallas kernels  29.9 us (75%)
  local copies, waits for them, and re-layouts  8.48 us (21%)
  other arithmetic  0.76 us (2%)
  between operations  0.65 us (2%)
    pallas_call x1, Pallas kernels, fused(): pl.pallas_call(functools.partial(fused_kernel, (groups, rows, span, lengt...  29.9 us
    unnamed x11, local copies, waits for them, and re-layouts  6.45 us

profile of v1, /device:TPU:0, one launch (start us, length us, event | category | flops | bytes accessed | tf_op | source)
XLA Modules:
  0.0 39.7 jit_solution(12253946347781381637)
XLA Ops:
  0.6 0.1 pad.2.clone
  0.7 0.8 %reshape.16 = f32[9,512]{1,0:T(8,128)S(1)} reshape(f32[3,3,512]{2,1,0:T(4,128)} %bitcast.6) | data formatting | bytes 36864 | tf_op jit(solution)/shard_map/reshape | solution.py:450
  1.5 0.8 %maximum_maximum_fusion.coef_hbm = f32[16,512]{1,0:T(8,128)S(1)} fusion(f32[1,512]{1,0:T(1,128)} %bitcast.8, f32[9,512]{1,0:T(8,128)S(1)} %reshape.16, f32[16]{0:T(128)S(1)} %pad.2.clone), kind=kLoop, calls=%fused_computation | loop fusion | flops 16384 | bytes 53312 | tf_op jit(solution)/shard_map/concatenate | solution.py:448
  2.2 0.0 copy-start
  2.2 1.6 %copy-done = bf16[2,512,1024]{2,1,0:T(8,128)(2,1)S(1)} copy-done((bf16[2,512,1024]{2,1,0:T(8,128)(2,1)S(1)}, bf16[2,512,1024]{2,1,0:T(8,128)(2,1)}, u32[]{:S(2)}) %copy-start) | copy-done | bytes 2097176
  3.8 0.0 copy-start.1
  3.8 1.0 %copy-done.1 = bf16[3,512,128]{2,1,0:T(8,128)(2,1)S(1)} copy-done((bf16[3,512,128]{2,1,0:T(8,128)(2,1)S(1)}, bf16[3,512,128]{2,1,0:T(8,128)(2,1)}, u32[]{:S(2)}) %copy-start.1) | copy-done | bytes 393240
  4.8 0.0 copy-start.2
  4.8 0.9 %copy-done.2 = bf16[512,128]{1,0:T(8,128)(2,1)S(1)} copy-done((bf16[512,128]{1,0:T(8,128)(2,1)S(1)}, bf16[512,128]{1,0:T(8,128)(2,1)}, u32[]{:S(2)}) %copy-start.2) | copy-done | bytes 131096
  5.7 0.0 copy-start.3
  5.7 0.9 %copy-done.3 = bf16[512,128]{1,0:T(8,128)(2,1)S(1)} copy-done((bf16[512,128]{1,0:T(8,128)(2,1)S(1)}, bf16[512,128]{1,0:T(8,128)(2,1)}, u32[]{:S(2)}) %copy-start.3) | copy-done | bytes 131096
  6.6 29.9 %shard_map.101 = (bf16[512,128]{1,0:T(8,128)(2,1)S(1)}, bf16[3,512,128]{2,1,0:T(8,128)(2,1)S(1)}, bf16[512,128]{1,0:T(8,128)(2,1)S(1)}, f32[16,512]{1,0:T(8,128)S(1)}) custom-call(bf16[3,512,128]{2,1,0:T(8,128)(2,1)S(1)} %copy-done.1, bf16[512,128]{1,0:T(8,128)(2,1)S(1)} %copy-done.2, bf16[512,128]{1,0:T(8,128)(2,1)S(1)} %copy-done.3, ...), custom_call_target="tpu_custom_call" | custom-call | tf_op jit(solution)/shard_map/pallas_call | solution.py:459
  36.5 0.6 %slice.7 = f32[1,512]{1,0:T(1,128)} slice(f32[16,512]{1,0:T(8,128)S(1)} %get-tuple-element.12), slice={[9:10], [0:512]} | slice | bytes 4096 | tf_op jit(solution)/shard_map/slice | solution.py:499
  37.1 0.6 %reshape.17 = f32[3,3,512]{2,1,0:T(4,128)} reshape(f32[9,512]{1,0:T(8,128)S(1)} %bitcast.5) | data formatting | bytes 36864 | tf_op jit(solution)/shard_map/reshape | solution.py:498
  37.7 0.7 %copy.14 = bf16[512,128]{1,0:T(8,128)(2,1)} copy(bf16[512,128]{1,0:T(8,128)(2,1)S(1)} %get-tuple-element.18) | data formatting | bytes 262144
  38.3 0.7 %copy.15 = bf16[3,512,128]{2,1,0:T(8,128)(2,1)} copy(bf16[3,512,128]{2,1,0:T(8,128)(2,1)S(1)} %get-tuple-element.19) | data formatting | bytes 786432
  39.1 0.7 %copy.16 = bf16[512,128]{1,0:T(8,128)(2,1)} copy(bf16[512,128]{1,0:T(8,128)(2,1)S(1)} %get-tuple-element.20) | data formatting | bytes 262144
  (1 shorter events, 0.0 us)
Async XLA Ops:
  2.2 1.6 %copy-start = (bf16[2,512,1024]{2,1,0:T(8,128)(2,1)S(1)}, bf16[2,512,1024]{2,1,0:T(8,128)(2,1)}, u32[]{:S(2)}) copy-start(bf16[2,512,1024]{2,1,0:T(8,128)(2,1)} %constant.4.clone.table_hbm) | copy-start | bytes 6291460
  3.8 1.0 %copy-start.1 = (bf16[3,512,128]{2,1,0:T(8,128)(2,1)S(1)}, bf16[3,512,128]{2,1,0:T(8,128)(2,1)}, u32[]{:S(2)}) copy-start(bf16[3,512,128]{2,1,0:T(8,128)(2,1)} %feat_hbm.1) | copy-start | bytes 1179652
  4.8 0.9 %copy-start.2 = (bf16[512,128]{1,0:T(8,128)(2,1)S(1)}, bf16[512,128]{1,0:T(8,128)(2,1)}, u32[]{:S(2)}) copy-start(bf16[512,128]{1,0:T(8,128)(2,1)} %cot_hbm.1) | copy-start | bytes 393220
  5.7 0.9 %copy-start.3 = (bf16[512,128]{1,0:T(8,128)(2,1)S(1)}, bf16[512,128]{1,0:T(8,128)(2,1)}, u32[]{:S(2)}) copy-start(bf16[512,128]{1,0:T(8,128)(2,1)} %filt_hbm.1) | copy-start | bytes 393220

commit v2 on v1

--- a/solution.py
+++ b/solution.py
@@ -11,7 +11,7 @@
 
 inner_length = 128
 radix_width = 8
-chunk_count = 1
+chunk_count = 2
 
 
 def phase_tables(row_count, col_count, length, direction):
@@ -144,13 +144,17 @@
     feat_hbm,
     cot_hbm,
     filt_hbm,
-    coef_hbm,
+    short_hbm,
+    gain_hbm,
     table_hbm,
     gated_hbm,
     grad_hbm,
     long_hbm,
-    small_hbm,
+    taps_hbm,
+    skip_hbm,
     table,
+    short_rows,
+    gain_line,
     coef_rows,
     coef_cols,
     arrived,
@@ -162,7 +166,8 @@
     back_time,
     results,
     sums,
-    sums_out,
+    taps_out,
+    skip_out,
     load_sem,
     own_in,
     own_out,
@@ -186,8 +191,9 @@
         return pl.ds(pl.multiple_of(start, chunk_rows), chunk_rows)
 
     loads = [
-        pltpu.make_async_copy(coef_hbm.at[:, at(me, rows)], coef_rows.at[0:16, :], load_sem.at[0]),
-        pltpu.make_async_copy(table_hbm, table, load_sem.at[1]),
+        pltpu.make_async_copy(short_hbm.at[:, :, at(me, rows)], short_rows, load_sem.at[0]),
+        pltpu.make_async_copy(gain_hbm, gain_line, load_sem.at[1]),
+        pltpu.make_async_copy(table_hbm, table, load_sem.at[2]),
     ]
     for load in loads:
         load.start()
@@ -195,21 +201,19 @@
     def in_pairs(owner, source, chunk):
         taken = chan_rows(owner, chunk)
         kept = pl.ds(chunk * chunk_rows, chunk_rows)
-        tokens = at(source, span)
         return [
-            (filt_hbm.at[taken, :], arrived.at[4, kept, tokens]),
-            (feat_hbm.at[:, taken, :], arrived.at[0:3, kept, tokens]),
-            (cot_hbm.at[taken, :], arrived.at[3, kept, tokens]),
+            (filt_hbm.at[taken, :], arrived.at[source, 4, kept, :]),
+            (feat_hbm.at[:, taken, :], arrived.at[source, 0:3, kept, :]),
+            (cot_hbm.at[taken, :], arrived.at[source, 3, kept, :]),
         ]
 
     def out_pairs(target, owner, chunk):
         kept = pl.ds(chunk * chunk_rows, chunk_rows)
         placed = chan_rows(owner, chunk)
-        tokens = at(target, span)
         return [
-            (results.at[0, kept, tokens], gated_hbm.at[placed, :]),
-            (results.at[1:4, kept, tokens], grad_hbm.at[:, placed, :]),
-            (results.at[4, kept, tokens], long_hbm.at[placed, :]),
+            (results.at[target, 0, kept, :], gated_hbm.at[placed, :]),
+            (results.at[target, 1:4, kept, :], grad_hbm.at[:, placed, :]),
+            (results.at[target, 4, kept, :], long_hbm.at[placed, :]),
         ]
 
     def remote(pair, send_sem, recv_sem, peer):
@@ -251,12 +255,29 @@
                 sent.append(copy)
 
     loads[0].wait()
-    coef_rows[16:, :] = jnp.zeros((coef_rows.shape[0] - 16, rows), jnp.float32)
+    loads[1].wait()
+    coef_rows[...] = jnp.zeros_like(coef_rows)
+    for stream in range(3):
+        coef_rows[stream * taps : (stream + 1) * taps, :] = short_rows[stream]
+    gain_row = jnp.zeros((1, rows), jnp.float32)
+    for group in range(groups):
+        part = gain_line[:, group * rows : (group + 1) * rows]
+        gain_row = gain_row + jnp.where(me == group, part, 0.0)
+    coef_rows[3 * taps : 3 * taps + 1, :] = gain_row
     coef_cols[...] = coef_rows[...].T
-    loads[1].wait()
-
-    group_rows = 16
+    loads[2].wait()
+
+    group_rows = 64
     scale = 1.0 / length
+
+    def tokens_of(kind, picked):
+        return jnp.concatenate([arrived[group, kind, picked, :] for group in range(groups)], 1)
+
+    def finish(kind, picked, values):
+        for group in range(groups):
+            results[group, kind, picked, :] = values[:, group * span : (group + 1) * span].astype(
+                jnp.bfloat16
+            )
 
     def column(index, picked):
         return coef_cols[picked, index : index + 1]
@@ -291,7 +312,7 @@
             picked = pl.ds(pl.multiple_of(base + step * group_rows, group_rows), group_rows)
             primed = []
             for stream in range(3):
-                wide = arrived[stream, picked, :].astype(jnp.float32)
+                wide = tokens_of(stream, picked).astype(jnp.float32)
                 running = column(stream * taps, picked) * wide
                 for offset in range(1, taps):
                     running = running + column(stream * taps + offset, picked) * delayed(
@@ -300,9 +321,9 @@
                 primed.append(running)
                 primed_buf[stream, inner, :] = running
             stacked[0, inner, :] = (primed[1] * primed[2]).astype(jnp.bfloat16)
-            cot_wide = arrived[3, picked, :].astype(jnp.float32)
+            cot_wide = tokens_of(3, picked).astype(jnp.float32)
             stacked[1, inner, :] = (cot_wide * primed[0]).astype(jnp.bfloat16)
-            stacked[2, inner, :] = arrived[4, picked, :]
+            stacked[2, inner, :] = tokens_of(4, picked)
 
         tile = 256
 
@@ -368,9 +389,9 @@
             mixed_back = (
                 (back_time[1, inner, :] + gain * gated).astype(jnp.bfloat16).astype(jnp.float32)
             )
-            results[4, picked, :] = back_time[2, inner, :].astype(jnp.bfloat16)
-            results[0, picked, :] = (primed_buf[0, inner, :] * long_wide).astype(jnp.bfloat16)
-            cot_wide = arrived[3, picked, :].astype(jnp.float32)
+            finish(4, picked, back_time[2, inner, :])
+            finish(0, picked, primed_buf[0, inner, :] * long_wide)
+            cot_wide = tokens_of(3, picked).astype(jnp.float32)
             primed_grad = [
                 cot_wide * long_wide,
                 mixed_back * primed_buf[2, inner, :],
@@ -380,7 +401,7 @@
             line = jnp.zeros((group_rows, sums.shape[1]), jnp.float32)
             for stream in range(3):
                 moving = primed_grad[stream]
-                wide = arrived[stream, picked, :].astype(jnp.float32)
+                wide = tokens_of(stream, picked).astype(jnp.float32)
                 running = column(stream * taps, picked) * moving
                 for offset in range(taps):
                     if offset:
@@ -389,7 +410,7 @@
                         )
                     total = jnp.sum(moving * delayed(wide, offset), axis=1, keepdims=True)
                     line = jnp.where(lane == stream * taps + offset, total, line)
-                results[1 + stream, picked, :] = running.astype(jnp.bfloat16)
+                finish(1 + stream, picked, running)
             total = jnp.sum(gated * mixed, axis=1, keepdims=True)
             sums[picked, :] = jnp.where(lane == 3 * taps, total, line)
 
@@ -406,24 +427,30 @@
             copy.start()
             own_copies.append(copy)
 
-    sums_out[...] = sums[...].T[0:16, :]
-    own_small = pltpu.make_async_copy(sums_out, small_hbm.at[:, at(me, rows)], small_own)
-    own_small.start()
-    for offset in range(1, groups):
-        peer = lax.rem(me + offset, groups)
-        copy = remote(
-            (sums_out, small_hbm.at[:, at(me, rows)]),
-            small_send.at[offset],
-            small_recv.at[offset],
-            peer,
-        )
+    turned_sums = sums[...].T
+    for stream in range(3):
+        taps_out[stream] = turned_sums[stream * taps : (stream + 1) * taps, :]
+    skip_out[...] = turned_sums[3 * taps : 3 * taps + 1, :]
+
+    def small_pairs(owner):
+        return [
+            (taps_out, taps_hbm.at[:, :, at(owner, rows)]),
+            (skip_out, skip_hbm.at[:, at(owner, rows)]),
+        ]
+
+    for kind, pair in enumerate(small_pairs(me)):
+        copy = pltpu.make_async_copy(pair[0], pair[1], small_own.at[kind])
         copy.start()
-        sent.append(copy)
+        own_copies.append(copy)
+        for offset in range(1, groups):
+            peer = lax.rem(me + offset, groups)
+            copy = remote(pair, small_send.at[kind, offset], small_recv.at[kind, offset], peer)
+            copy.start()
+            sent.append(copy)
     for copy in sent:
         copy.wait_send()
     for copy in own_copies[3 * chunks :]:
         copy.wait()
-    own_small.wait()
     for offset in range(1, groups):
         source = lax.rem(me + groups - offset, groups)
         for chunk in range(chunks):
@@ -431,12 +458,10 @@
                 remote(
                     pair, out_send.at[chunk, kind, offset], out_recv.at[chunk, kind, offset], source
                 ).wait_recv()
-        remote(
-            (sums_out, small_hbm.at[:, at(source, rows)]),
-            small_send.at[offset],
-            small_recv.at[offset],
-            source,
-        ).wait_recv()
+        for kind, pair in enumerate(small_pairs(source)):
+            remote(
+                pair, small_send.at[kind, offset], small_recv.at[kind, offset], source
+            ).wait_recv()
 
 
 def fused(features, cotangent, long_filter, short_filters, skip_gain, groups, chunks):
@@ -445,58 +470,60 @@
     length = span * groups
     taps = short_filters.shape[2]
     chunk_rows = rows // chunks
-    coef = jnp.concatenate(
-        [
-            jnp.swapaxes(short_filters, 1, 2).reshape(3 * taps, channels),
-            skip_gain[None],
-            jnp.zeros((15 - 3 * taps, channels), jnp.float32),
-        ],
-        0,
-    )
-    hbm = pl.BlockSpec(memory_space=pl.ANY)
+    hbm = pl.BlockSpec(memory_space=pltpu.HBM)
     dma = pltpu.SemaphoreType.DMA
     narrow = jnp.bfloat16
-    gated_out, feature_grad, long_grad, small = pl.pallas_call(
+    gated_out, feature_grad, long_grad, taps_grad, gain_grad = pl.pallas_call(
         functools.partial(fused_kernel, (groups, rows, span, length, taps, chunks)),
         out_shape=(
             jax.ShapeDtypeStruct((channels, span), narrow),
             jax.ShapeDtypeStruct((3, channels, span), narrow),
             jax.ShapeDtypeStruct((channels, span), narrow),
-            jax.ShapeDtypeStruct((16, channels), jnp.float32),
+            jax.ShapeDtypeStruct((3, taps, channels), jnp.float32),
+            jax.ShapeDtypeStruct((1, channels), jnp.float32),
         ),
-        in_specs=[hbm] * 5,
-        out_specs=(hbm,) * 4,
+        in_specs=[hbm] * 6,
+        out_specs=(hbm,) * 5,
         scratch_shapes=[
             pltpu.VMEM((2, length, 2 * length), narrow),
+            pltpu.VMEM((3, taps, rows), jnp.float32),
+            pltpu.VMEM((1, channels), jnp.float32),
             pltpu.VMEM((rows, rows), jnp.float32),
             pltpu.VMEM((rows, rows), jnp.float32),
-            pltpu.VMEM((5, rows, length), narrow),
+            pltpu.VMEM((groups, 5, rows, span), narrow),
             pltpu.VMEM((3, chunk_rows, length), narrow),
             pltpu.VMEM((3, chunk_rows, length), jnp.float32),
             pltpu.VMEM((3, chunk_rows, 2 * length), jnp.float32),
             pltpu.VMEM((3, chunk_rows, 2 * length), narrow),
             pltpu.VMEM((3, chunk_rows, 2 * length), narrow),
             pltpu.VMEM((3, chunk_rows, length), jnp.float32),
-            pltpu.VMEM((5, rows, length), narrow),
+            pltpu.VMEM((groups, 5, rows, span), narrow),
             pltpu.VMEM((rows, rows), jnp.float32),
-            pltpu.VMEM((16, rows), jnp.float32),
-            dma((2,)),
+            pltpu.VMEM((3, taps, rows), jnp.float32),
+            pltpu.VMEM((1, rows), jnp.float32),
+            dma((3,)),
             dma((chunks, 3)),
             dma((chunks, 3)),
             dma((chunks, 3, groups)),
             dma((chunks, 3, groups)),
             dma((chunks, 3, groups)),
             dma((chunks, 3, groups)),
-            dma,
-            dma((groups,)),
-            dma((groups,)),
+            dma((2,)),
+            dma((2, groups)),
+            dma((2, groups)),
         ],
         compiler_params=pltpu.CompilerParams(
-            collective_id=0, has_side_effects=True, vmem_limit_bytes=48 * 1024 * 1024
+            collective_id=0, has_side_effects=True
         ),
-    )(features, cotangent, long_filter, coef, packed_tables(length))
-    short_grad = jnp.swapaxes(small[: 3 * taps].reshape(3, taps, channels), 1, 2)
-    return gated_out, feature_grad, long_grad, short_grad, small[3 * taps]
+    )(
+        features,
+        cotangent,
+        long_filter,
+        jnp.swapaxes(short_filters, 1, 2),
+        skip_gain[None],
+        packed_tables(length),
+    )
+    return gated_out, feature_grad, long_grad, jnp.swapaxes(taps_grad, 1, 2), gain_grad[0]
 
 
 def dense_fits(features, short_filters, groups):

time: 40.1 us -> 31.8 us (0.79)
  Pallas kernels: 29.9 us -> 23.4 us
  local copies, waits for them, and re-layouts: 8.48 us -> 7.49 us
  other arithmetic: 0.76 us -> 0 us
    pallas_call x1, Pallas kernels: 29.9 us -> 23.4 us  [fused(): pl.pallas_call(functools.partial(fused_kernel, (groups, rows, span, lengt...]
    reshape x2 -> x0, local copies, waits for them, and re-layouts: 1.37 us -> none  [the longest x1 0.75 us: fused(): jnp.swapaxes(short_filters, 1, 2).reshape(3 * taps, channels)]
    unnamed x11 -> x5, local copies, waits for them, and re-layouts: 6.45 us -> 7.49 us
    concatenate x1 -> x0, other arithmetic: 0.76 us -> none  [fused(): jnp.concatenate([jnp.swapaxes(short_filters, 1, 2).reshape(3 * taps, chan...]
    slice x1 -> x0, local copies, waits for them, and re-layouts: 0.58 us -> none  [fused(): return (gated_out, feature_grad, long_grad, short_grad, small[3 * taps])]
where the time goes in v2:
time: 31.8 us; the launch traced here: 31.6 us
  Pallas kernels  23.4 us (74%)
  local copies, waits for them, and re-layouts  7.49 us (24%)
  between operations  0.64 us (2%)
    pallas_call x1, Pallas kernels, fused(): pl.pallas_call(functools.partial(fused_kernel, (groups, rows, span, lengt...  23.4 us
    unnamed x5, local copies, waits for them, and re-layouts  7.49 us

profile of v2, /device:TPU:0, one launch (start us, length us, event | category | flops | bytes accessed | tf_op | source)
XLA Modules:
  0.0 31.6 jit_solution(3953978675538280217)
XLA Ops:
  0.6 23.4 %shard_map.101 = (bf16[512,128]{1,0:T(8,128)(2,1)}, bf16[3,512,128]{2,1,0:T(8,128)(2,1)}, bf16[512,128]{1,0:T(8,128)(2,1)}, f32[3,3,512]{2,1,0:T(4,128)}, f32[1,512]{1,0:T(1,128)}) custom-call(bf16[3,512,128]{2,1,0:T(8,128)(2,1)} %feat_hbm.1, bf16[512,128]{1,0:T(8,128)(2,1)} %cot_hbm.1, bf16[512,128]{1,0:T(8,128)(2,1)} %filt_hbm.1, f32[3,3,512]{2,1,0:T(4,128)} %bitcast.4, ...), custom_call_target="tpu_custom_call" | custom-call | tf_op jit(solution)/shard_map/pallas_call | solution.py:476
  24.1 1.6 %copy.16 = bf16[512,128]{1,0:T(8,128)(2,1)} copy(bf16[512,128]{1,0:T(8,128)(2,1)} %get-tuple-element.20) | data formatting | bytes 262144
  25.6 1.8 %copy.17 = bf16[3,512,128]{2,1,0:T(8,128)(2,1)} copy(bf16[3,512,128]{2,1,0:T(8,128)(2,1)} %get-tuple-element.21) | data formatting | bytes 786432
  27.4 1.6 %copy.18 = bf16[512,128]{1,0:T(8,128)(2,1)} copy(bf16[512,128]{1,0:T(8,128)(2,1)} %get-tuple-element.22) | data formatting | bytes 262144
  29.0 1.3 %copy.19 = f32[3,512,3]{1,2,0:T(4,128)} copy(f32[3,512,3]{1,2,0:T(4,128)} %bitcast.5) | data formatting | bytes 36864
  30.3 1.2 %copy.20 = f32[512]{0:T(512)} copy(f32[512]{0:T(512)} %bitcast.7) | data formatting | bytes 4096

commit v3 on v2

--- a/solution.py
+++ b/solution.py
@@ -325,7 +325,7 @@
             stacked[1, inner, :] = (cot_wide * primed[0]).astype(jnp.bfloat16)
             stacked[2, inner, :] = tokens_of(4, picked)
 
-        tile = 256
+        tile = 512
 
         @pl.loop(0, 2 * length // tile)
         def _(step):
@@ -464,6 +464,28 @@
             ).wait_recv()
 
 
+def settle_kernel(*refs):
+    count = len(refs) // 2
+    finished = refs[2 * count]
+    copies = []
+    for index in range(count):
+        copy = pltpu.make_async_copy(refs[index], refs[count + index], finished.at[index])
+        copy.start()
+        copies.append(copy)
+    for copy in copies:
+        copy.wait()
+
+
+def settle(values):
+    return pl.pallas_call(
+        settle_kernel,
+        out_shape=tuple(jax.ShapeDtypeStruct(value.shape, value.dtype) for value in values),
+        in_specs=[pl.BlockSpec(memory_space=pltpu.VMEM)] * len(values),
+        out_specs=(pl.BlockSpec(memory_space=pltpu.HBM),) * len(values),
+        scratch_shapes=[pltpu.SemaphoreType.DMA((len(values),))],
+    )(*values)
+
+
 def fused(features, cotangent, long_filter, short_filters, skip_gain, groups, chunks):
     channels, span = cotangent.shape
     rows = channels // groups
@@ -473,7 +495,7 @@
     hbm = pl.BlockSpec(memory_space=pltpu.HBM)
     dma = pltpu.SemaphoreType.DMA
     narrow = jnp.bfloat16
-    gated_out, feature_grad, long_grad, taps_grad, gain_grad = pl.pallas_call(
+    outputs = pl.pallas_call(
         functools.partial(fused_kernel, (groups, rows, span, length, taps, chunks)),
         out_shape=(
             jax.ShapeDtypeStruct((channels, span), narrow),
@@ -483,7 +505,7 @@
             jax.ShapeDtypeStruct((1, channels), jnp.float32),
         ),
         in_specs=[hbm] * 6,
-        out_specs=(hbm,) * 5,
+        out_specs=(pl.BlockSpec(memory_space=pltpu.VMEM),) * 5,
         scratch_shapes=[
             pltpu.VMEM((2, length, 2 * length), narrow),
             pltpu.VMEM((3, taps, rows), jnp.float32),
@@ -523,6 +545,7 @@
         skip_gain[None],
         packed_tables(length),
     )
+    gated_out, feature_grad, long_grad, taps_grad, gain_grad = settle(outputs)
     return gated_out, feature_grad, long_grad, jnp.swapaxes(taps_grad, 1, 2), gain_grad[0]
 
 
@@ -533,7 +556,7 @@
         channels % groups == 0
         and rows % 128 == 0
         and span % 128 == 0
-        and length % 256 == 0
+        and length % 512 == 0
         and length <= 1024
         and rows <= 256
         and 3 * short_filters.shape[2] < 16

time: 31.8 us -> 25.4 us (0.80)
  local copies, waits for them, and re-layouts: 7.49 us -> 0 us
  Pallas kernels: 23.4 us -> 24.6 us
    unnamed x5 -> x0, local copies, waits for them, and re-layouts: 7.49 us -> none
    pallas_call x0 -> x1, Pallas kernels: none -> 1.98 us  [settle(): pl.pallas_call(settle_kernel, out_shape=tuple((jax.ShapeDtypeStruct(value...]
    pallas_call x1, Pallas kernels: 23.4 us -> 22.6 us  [fused(): pl.pallas_call(functools.partial(fused_kernel, (groups, rows, span, lengt...]
where the time goes in v3:
time: 25.4 us; the launch traced here: 25.2 us
  Pallas kernels  24.6 us (97%)
  between operations  0.64 us (3%)
    pallas_call x1, Pallas kernels, fused(): pl.pallas_call(functools.partial(fused_kernel, (groups, rows, span, lengt...  22.6 us
    pallas_call x1, Pallas kernels, settle(): pl.pallas_call(settle_kernel, out_shape=tuple((jax.ShapeDtypeStruct(value...  1.98 us

profile of v3, /device:TPU:0, one launch (start us, length us, event | category | flops | bytes accessed | tf_op | source)
XLA Modules:
  0.0 25.2 jit_solution(15236078261880952366)
XLA Ops:
  0.6 22.6 %shard_map.101 = (bf16[512,128]{1,0:T(8,128)(2,1)}, bf16[3,512,128]{2,1,0:T(8,128)(2,1)}, bf16[512,128]{1,0:T(8,128)(2,1)}, f32[3,3,512]{2,1,0:T(4,128)}, f32[1,512]{1,0:T(1,128)}) custom-call(bf16[3,512,128]{2,1,0:T(8,128)(2,1)} %feat_hbm.1, bf16[512,128]{1,0:T(8,128)(2,1)} %cot_hbm.1, bf16[512,128]{1,0:T(8,128)(2,1)} %filt_hbm.1, f32[3,3,512]{2,1,0:T(4,128)} %bitcast.4, ...), custom_call_target="tpu_custom_call" | custom-call | tf_op jit(solution)/shard_map/pallas_call | solution.py:498
  23.3 2.0 %shard_map.102 = (bf16[512,128]{1,0:T(8,128)(2,1)}, bf16[3,512,128]{2,1,0:T(8,128)(2,1)}, bf16[512,128]{1,0:T(8,128)(2,1)}, f32[3,3,512]{2,1,0:T(4,128)}, f32[1,512]{1,0:T(1,128)}) custom-call(bf16[512,128]{1,0:T(8,128)(2,1)} %get-tuple-element.15.refs_0_, bf16[3,512,128]{2,1,0:T(8,128)(2,1)} %get-tuple-element.16.refs_1_, ...), custom_call_target="tpu_custom_call" | custom-call | tf_op jit(solution)/shard_map/pallas_call | solution.py:480

commit v4 on v3

--- a/solution.py
+++ b/solution.py
@@ -161,8 +161,7 @@
     stacked,
     primed_buf,
     freq,
-    back_high,
-    back_low,
+    back_both,
     back_time,
     results,
     sums,
@@ -190,6 +189,14 @@
         start = owner * rows + chunk * chunk_rows
         return pl.ds(pl.multiple_of(start, chunk_rows), chunk_rows)
 
+    barrier = pltpu.get_barrier_semaphore()
+    for offset in range(1, groups):
+        pl.semaphore_signal(
+            barrier,
+            inc=1,
+            device_id={"seq": lax.rem(me + offset, groups)},
+            device_id_type=pl.DeviceIdType.MESH,
+        )
     loads = [
         pltpu.make_async_copy(short_hbm.at[:, :, at(me, rows)], short_rows, load_sem.at[0]),
         pltpu.make_async_copy(gain_hbm, gain_line, load_sem.at[1]),
@@ -233,14 +240,6 @@
             copy.start()
             own_copies.append(copy)
 
-    barrier = pltpu.get_barrier_semaphore()
-    for offset in range(1, groups):
-        pl.semaphore_signal(
-            barrier,
-            inc=1,
-            device_id={"seq": lax.rem(me + offset, groups)},
-            device_id_type=pl.DeviceIdType.MESH,
-        )
     pl.semaphore_wait(barrier, groups - 1)
 
     sent = []
@@ -294,6 +293,20 @@
         lane = lax.broadcasted_iota(jnp.int32, values.shape, 1)
         moved = pltpu.roll(values, length - offset, 1)
         return jnp.where(lane < length - offset, moved, 0.0)
+
+    def send_kinds(chunk, kinds):
+        for offset in range(1, groups):
+            peer = lax.rem(me + offset, groups)
+            pairs = out_pairs(peer, me, chunk)
+            for kind in kinds:
+                copy = remote(
+                    pairs[kind],
+                    out_send.at[chunk, kind, offset],
+                    out_recv.at[chunk, kind, offset],
+                    peer,
+                )
+                copy.start()
+                sent.append(copy)
 
     for chunk in range(chunks):
         base = chunk * chunk_rows
@@ -352,8 +365,8 @@
                     value = part * weight
                     high = value.astype(jnp.bfloat16)
                     low = (value - high.astype(jnp.float32)).astype(jnp.bfloat16)
-                    back_high[slot, inner, half * length : (half + 1) * length] = high
-                    back_low[slot, inner, half * length : (half + 1) * length] = low
+                    back_both[slot, inner, half * length : (half + 1) * length] = high
+                    back_both[3 + slot, inner, half * length : (half + 1) * length] = low
 
             put(0, mix_c, mix_s, kern_c, kern_s, -1.0)
             put(1, grad_c, grad_s, kern_c, kern_s, 1.0)
@@ -362,19 +375,20 @@
         @pl.loop(0, length // tile)
         def _(step):
             picked = pl.ds(pl.multiple_of(step * tile, tile), tile)
-            high = back_high[...].reshape(3 * chunk_rows, 2 * length)
-            low = back_low[...].reshape(3 * chunk_rows, 2 * length)
+            both = back_both[...].reshape(6 * chunk_rows, 2 * length)
+            high = both[: 3 * chunk_rows]
             turned = (((1,), (1,)), ((), ()))
-            total = lax.dot_general(
-                high, table[0, picked, :], turned, preferred_element_type=jnp.float32
+            pair = lax.dot_general(
+                both, table[0, picked, :], turned, preferred_element_type=jnp.float32
             )
-            total += lax.dot_general(
-                low, table[0, picked, :], turned, preferred_element_type=jnp.float32
-            )
+            total = pair[: 3 * chunk_rows] + pair[3 * chunk_rows :]
             total += lax.dot_general(
                 high, table[1, picked, :], turned, preferred_element_type=jnp.float32
             )
             back_time[:, :, picked] = total.reshape(3, chunk_rows, tile)
+
+        finish(4, pl.ds(base, chunk_rows), back_time[2])
+        send_kinds(chunk, (2,))
 
         @pl.loop(0, chunk_rows // group_rows)
         def _(step):
@@ -389,7 +403,6 @@
             mixed_back = (
                 (back_time[1, inner, :] + gain * gated).astype(jnp.bfloat16).astype(jnp.float32)
             )
-            finish(4, picked, back_time[2, inner, :])
             finish(0, picked, primed_buf[0, inner, :] * long_wide)
             cot_wide = tokens_of(3, picked).astype(jnp.float32)
             primed_grad = [
@@ -414,14 +427,7 @@
             total = jnp.sum(gated * mixed, axis=1, keepdims=True)
             sums[picked, :] = jnp.where(lane == 3 * taps, total, line)
 
-        for offset in range(1, groups):
-            peer = lax.rem(me + offset, groups)
-            for kind, pair in enumerate(out_pairs(peer, me, chunk)):
-                copy = remote(
-                    pair, out_send.at[chunk, kind, offset], out_recv.at[chunk, kind, offset], peer
-                )
-                copy.start()
-                sent.append(copy)
+        send_kinds(chunk, (0, 1))
         for kind, pair in enumerate(out_pairs(me, me, chunk)):
             copy = pltpu.make_async_copy(pair[0], pair[1], own_out.at[chunk, kind])
             copy.start()
@@ -516,8 +522,7 @@
             pltpu.VMEM((3, chunk_rows, length), narrow),
             pltpu.VMEM((3, chunk_rows, length), jnp.float32),
             pltpu.VMEM((3, chunk_rows, 2 * length), jnp.float32),
-            pltpu.VMEM((3, chunk_rows, 2 * length), narrow),
-            pltpu.VMEM((3, chunk_rows, 2 * length), narrow),
+            pltpu.VMEM((6, chunk_rows, 2 * length), narrow),
             pltpu.VMEM((3, chunk_rows, length), jnp.float32),
             pltpu.VMEM((groups, 5, rows, span), narrow),
             pltpu.VMEM((rows, rows), jnp.float32),

time: 25.4 us -> 24.6 us (0.969)
  Pallas kernels: 24.6 us -> 23.8 us
    pallas_call x1, Pallas kernels: 22.6 us -> 21.8 us  [fused(): pl.pallas_call(functools.partial(fused_kernel, (groups, rows, span, lengt...]
where the time goes in v4:
time: 24.6 us; the launch traced here: 24.4 us
  Pallas kernels  23.8 us (97%)
  between operations  0.64 us (3%)
    pallas_call x1, Pallas kernels, fused(): pl.pallas_call(functools.partial(fused_kernel, (groups, rows, span, lengt...  21.8 us
    pallas_call x1, Pallas kernels, settle(): pl.pallas_call(settle_kernel, out_shape=tuple((jax.ShapeDtypeStruct(value...  1.98 us

profile of v4, /device:TPU:0, one launch (start us, length us, event | category | flops | bytes accessed | tf_op | source)
XLA Modules:
  0.0 24.4 jit_solution(8563607344831501331)
XLA Ops:
  0.6 21.8 %shard_map.101 = (bf16[512,128]{1,0:T(8,128)(2,1)}, bf16[3,512,128]{2,1,0:T(8,128)(2,1)}, bf16[512,128]{1,0:T(8,128)(2,1)}, f32[3,3,512]{2,1,0:T(4,128)}, f32[1,512]{1,0:T(1,128)}) custom-call(bf16[3,512,128]{2,1,0:T(8,128)(2,1)} %feat_hbm.1, bf16[512,128]{1,0:T(8,128)(2,1)} %cot_hbm.1, bf16[512,128]{1,0:T(8,128)(2,1)} %filt_hbm.1, f32[3,3,512]{2,1,0:T(4,128)} %bitcast.4, ...), custom_call_target="tpu_custom_call" | custom-call | tf_op jit(solution)/shard_map/pallas_call | solution.py:504
  22.5 2.0 %shard_map.102 = (bf16[512,128]{1,0:T(8,128)(2,1)}, bf16[3,512,128]{2,1,0:T(8,128)(2,1)}, bf16[512,128]{1,0:T(8,128)(2,1)}, f32[3,3,512]{2,1,0:T(4,128)}, f32[1,512]{1,0:T(1,128)}) custom-call(bf16[512,128]{1,0:T(8,128)(2,1)} %get-tuple-element.15.refs_0_, bf16[3,512,128]{2,1,0:T(8,128)(2,1)} %get-tuple-element.16.refs_1_, ...), custom_call_target="tpu_custom_call" | custom-call | tf_op jit(solution)/shard_map/pallas_call | solution.py:486

commit v5 on v4

--- a/solution.py
+++ b/solution.py
@@ -389,6 +389,11 @@
 
         finish(4, pl.ds(base, chunk_rows), back_time[2])
         send_kinds(chunk, (2,))
+        whole = pl.ds(base, chunk_rows)
+        with_gain = back_time[0] + column(3 * taps, whole) * stacked[0].astype(jnp.float32)
+        back_time[0] = with_gain.astype(jnp.bfloat16).astype(jnp.float32)
+        finish(0, whole, primed_buf[0] * back_time[0])
+        send_kinds(chunk, (0,))
 
         @pl.loop(0, chunk_rows // group_rows)
         def _(step):
@@ -397,13 +402,10 @@
             mixed = stacked[0, inner, :].astype(jnp.float32)
             gated = stacked[1, inner, :].astype(jnp.float32)
             gain = column(3 * taps, picked)
-            long_wide = (
-                (back_time[0, inner, :] + gain * mixed).astype(jnp.bfloat16).astype(jnp.float32)
-            )
+            long_wide = back_time[0, inner, :]
             mixed_back = (
                 (back_time[1, inner, :] + gain * gated).astype(jnp.bfloat16).astype(jnp.float32)
             )
-            finish(0, picked, primed_buf[0, inner, :] * long_wide)
             cot_wide = tokens_of(3, picked).astype(jnp.float32)
             primed_grad = [
                 cot_wide * long_wide,
@@ -427,7 +429,7 @@
             total = jnp.sum(gated * mixed, axis=1, keepdims=True)
             sums[picked, :] = jnp.where(lane == 3 * taps, total, line)
 
-        send_kinds(chunk, (0, 1))
+        send_kinds(chunk, (1,))
         for kind, pair in enumerate(out_pairs(me, me, chunk)):
             copy = pltpu.make_async_copy(pair[0], pair[1], own_out.at[chunk, kind])
             copy.start()

time: 24.6 us -> 24.3 us (0.988)
  Pallas kernels: 23.8 us -> 23.5 us
    pallas_call x1, Pallas kernels: 21.8 us -> 21.6 us  [fused(): pl.pallas_call(functools.partial(fused_kernel, (groups, rows, span, lengt...]
where the time goes in v5:
time: 24.3 us; the launch traced here: 24.2 us
  Pallas kernels  23.5 us (97%)
  between operations  0.64 us (3%)
    pallas_call x1, Pallas kernels, fused(): pl.pallas_call(functools.partial(fused_kernel, (groups, rows, span, lengt...  21.6 us
    pallas_call x1, Pallas kernels, settle(): pl.pallas_call(settle_kernel, out_shape=tuple((jax.ShapeDtypeStruct(value...  1.98 us

profile of v5, /device:TPU:0, one launch (start us, length us, event | category | flops | bytes accessed | tf_op | source)
XLA Modules:
  0.0 24.2 jit_solution(18442813601806664484)
XLA Ops:
  0.6 21.6 %shard_map.101 = (bf16[512,128]{1,0:T(8,128)(2,1)}, bf16[3,512,128]{2,1,0:T(8,128)(2,1)}, bf16[512,128]{1,0:T(8,128)(2,1)}, f32[3,3,512]{2,1,0:T(4,128)}, f32[1,512]{1,0:T(1,128)}) custom-call(bf16[3,512,128]{2,1,0:T(8,128)(2,1)} %feat_hbm.1, bf16[512,128]{1,0:T(8,128)(2,1)} %cot_hbm.1, bf16[512,128]{1,0:T(8,128)(2,1)} %filt_hbm.1, f32[3,3,512]{2,1,0:T(4,128)} %bitcast.4, ...), custom_call_target="tpu_custom_call" | custom-call | tf_op jit(solution)/shard_map/pallas_call | solution.py:506
  22.2 2.0 %shard_map.102 = (bf16[512,128]{1,0:T(8,128)(2,1)}, bf16[3,512,128]{2,1,0:T(8,128)(2,1)}, bf16[512,128]{1,0:T(8,128)(2,1)}, f32[3,3,512]{2,1,0:T(4,128)}, f32[1,512]{1,0:T(1,128)}) custom-call(bf16[512,128]{1,0:T(8,128)(2,1)} %get-tuple-element.15.refs_0_, bf16[3,512,128]{2,1,0:T(8,128)(2,1)} %get-tuple-element.16.refs_1_, ...), custom_call_target="tpu_custom_call" | custom-call | tf_op jit(solution)/shard_map/pallas_call | solution.py:488
